TPU v7x, 512 devices: a whole 4x8x8 slice. The times are simulated.
512 devices in a mesh: space: 64 (over z, x, y_lo), sta: 8 (over y_hi, core).
Axes of the slice: x: 4, y: 8 (y_hi: 4, y_lo: 2; y = y_hi * 2 + y_lo), z: 8, core: 2. Of those that a mesh axis runs over, the one named last changes fastest.
Arguments:
- coarse_times: float32 [16, 320, 32, 128], P('sta', 'space'), as said below
- model_map: int32 [320, 32, 128], P('space'), may hold values from 0 to 63
- slowness: float32 [64], replicated, may hold values from 0.12 to 0.3
- picks: float32 [256, 16], replicated
- pick_mask: int32 [256, 16], replicated, may hold values from 0 to 1, as said below
Outputs:
- refined: float32 [16, 320, 32, 128], P(None, 'space', 'sta')
- density: float32 [256, 320, 32, 128], P(None, 'space', 'sta')
Inputs may be any that keep to these rules, and one draw needn't show every extreme that they name: `pick_mask`: each event has at least 4 stations with a pick. `coarse_times`: zero at each station's own cell and positive elsewhere.
All inputs are finite; a program needn't handle non-finite values.
Results may differ from a plain program's by a relative error of at most 0.0003.
Values sent between devices are 32-bit elements; how exact they have to be, the bound alone decides.
A program may use at most 64 MiB of HBM per device.

v0:
```python
import jax
import jax.numpy as jnp
from jax import lax
from jax.sharding import PartitionSpec as P

ROUNDS = 12
BIG = 1000000.0
pick_sigma = 0.25
grid_step = 1.0
block_events = 32


def extended_2(block, sides, width):
    for axis, dim in sides:
        count = lax.axis_size(axis)
        forward = [(i, i + 1) for i in range(count - 1)]
        backward = [(target, source) for source, target in forward]
        low = lax.ppermute(
            lax.slice_in_dim(block, block.shape[dim] - width, None, axis=dim), axis, forward
        )
        high = lax.ppermute(lax.slice_in_dim(block, 0, width, axis=dim), axis, backward)
        block = jnp.concatenate([low, block, high], axis=dim)
    return block


def godunov(near_one, near_two, near_three, speed):
    lowest = jnp.minimum(jnp.minimum(near_one, near_two), near_three)
    highest = jnp.maximum(jnp.maximum(near_one, near_two), near_three)
    middle = jnp.maximum(
        jnp.minimum(near_one, near_two), jnp.minimum(jnp.maximum(near_one, near_two), near_three)
    )
    gap_mid = middle - lowest
    gap_high = highest - lowest
    two_sided = 0.5 * (
        gap_mid + jnp.sqrt(jnp.maximum(2.0 * speed * speed - gap_mid * gap_mid, 0.0))
    )
    gap_sum = gap_mid + gap_high
    squares = gap_mid * gap_mid + gap_high * gap_high - speed * speed
    three_sided = (gap_sum + jnp.sqrt(jnp.maximum(gap_sum * gap_sum - 3.0 * squares, 0.0))) / 3.0
    increase = jnp.where(
        speed <= gap_mid, speed, jnp.where(two_sided <= gap_high, two_sided, three_sided)
    )
    return lowest + increase


def relax(extended, speed):
    centre = extended[:, 1:-1]
    along_x = jnp.minimum(extended[:, :-2], extended[:, 2:])
    padded = jnp.pad(centre, ((0, 0), (0, 0), (1, 1), (1, 1)), constant_values=BIG)
    along_y = jnp.minimum(padded[:, :, :-2, 1:-1], padded[:, :, 2:, 1:-1])
    along_z = jnp.minimum(padded[:, :, 1:-1, :-2], padded[:, :, 1:-1, 2:])
    return jnp.minimum(centre, godunov(along_x, along_y, along_z, speed[None]))


def close_rims(extended, rim_width, at_lower, at_upper):
    cell_count = extended.shape[1]
    position = lax.broadcasted_iota(jnp.int32, (1, cell_count, 1, 1), 1)
    outside = (position < rim_width) & at_lower | (position >= cell_count - rim_width) & at_upper
    return jnp.where(outside, BIG, extended)


def misfit_block(event_pair, flat_tables):
    arrivals, observed = event_pair
    pick_count = jnp.sum(observed, 1)
    residual = arrivals[:, :, None] - flat_tables[None]
    anchor_shift = jnp.sum(observed[:, :, None] * residual, 1) / pick_count[:, None]
    deviation = residual - anchor_shift[:, None, :]
    return jnp.sum(observed[:, :, None] * deviation * deviation, 1)


def body(coarse_times, model_map, slowness, picks, pick_mask):
    levels = lax.broadcasted_iota(jnp.int32, (slowness.shape[0], 1, 1, 1), 0)
    speed = grid_step * jnp.sum(
        jnp.where(model_map[None] == levels, slowness[:, None, None, None], 0.0), 0
    )
    position_space = lax.axis_index("space")
    devices_space = lax.axis_size("space")
    at_lower = position_space == 0
    at_upper = position_space == devices_space - 1
    tables = coarse_times

    def one_round(round_index, tables):
        extended = extended_2(tables, (("space", 1),), 1)
        return relax(close_rims(extended, 1, at_lower, at_upper), speed)

    tables = lax.fori_loop(0, ROUNDS, one_round, tables)
    refined = lax.all_to_all(tables, "sta", split_axis=2, concat_axis=0, tiled=True)
    stations = refined.shape[0]
    flat_tables = refined.reshape(stations, -1)
    observed = pick_mask.astype(jnp.float32)
    blocks = lax.map(
        lambda event_pair: misfit_block(event_pair, flat_tables),
        (picks.reshape(-1, block_events, stations), observed.reshape(-1, block_events, stations)),
    )
    score = -0.5 * blocks.reshape(picks.shape[0], -1) / (pick_sigma * pick_sigma)
    local_top = jnp.max(score, 1)
    top_score = lax.pmax(local_top, ("space", "sta"))
    cell_weights = jnp.exp(score - top_score[:, None])
    mass_sum = lax.psum(jnp.sum(cell_weights, 1), ("space", "sta"))
    density = cell_weights / mass_sum[:, None]
    density = density.reshape(picks.shape[0], refined.shape[1], refined.shape[2], refined.shape[3])
    return (refined, density)


def solution(mesh):
    placed = (P("sta", "space", None, None), P("space", None, None), P(), P(), P())
    return jax.shard_map(
        body,
        mesh=mesh,
        in_specs=placed,
        out_specs=(P(None, "space", "sta", None), P(None, "space", "sta", None)),
        check_vma=False,
    )
```

profile of v0, /device:TPU:1, one launch (start us, length us, event | category | flops | bytes accessed | tf_op | source)
XLA Modules:
  0.0 400.3 jit_solution(15108687910519187585)
XLA Ops:
  0.6 0.9 copy.54
  1.5 1.5 select_reduce_fusion
  3.1 96.4 %while.22 = (s32[]{:T(128)}, f32[2,5,32,128]{3,2,1,0:T(8,128)S(1)}, pred[]{:T(512)}, pred[]{:T(512)}, f32[5,32,128]{2,1,0:T(8,128)S(1)}, /*index=5*/f32[1,5,32,128]{3,2,1,0:T(8,128)S(1)}, s32[]{:T(128)}) while((s32[]{:T(128)}, f32[2,5,32,128]{3,2,1,0:T(8,128)S(1)}, pred[]{:T(512)}, pred[]{:T(512)}, f32[5,32,128]{2,1,0:T(8,128)S(1)}, ...), condition=%wide.region_2.3_spmd, body=%wide.region_1.2_spmd.sunk | while | flops 1523749 | bytes 2244781 | solution.py:86
  3.1 1.3 collective-permute-start
  4.4 4.6 %collective-permute-start.1 = (f32[2,1,32,128]{3,2,1,0:T(8,128)S(1)}, f32[2,1,32,128]{3,2,1,0:T(8,128)S(1)}, u32[]{:S(2)}, u32[]{:S(2)}) collective-permute-start(f32[2,1,32,128]{3,2,1,0:T(8,128)S(1)} %get-tuple-element.226), channel_id=1, source_target_pairs={{0,8},{8,16},{16,24},{24,32},{32,40},{40,48},{48,56},{56,64},{64,7... | collective-permute-start | bytes 98312 | tf_op jit(solution)/shard_map/while/body/eval_jaxpr/ppermute | solution.py:18
  9.1 1.0 collective-permute-done.1
  10.6 1.3 collective-permute-start
  11.9 4.9 %collective-permute-start.1 = (f32[2,1,32,128]{3,2,1,0:T(8,128)S(1)}, f32[2,1,32,128]{3,2,1,0:T(8,128)S(1)}, u32[]{:S(2)}, u32[]{:S(2)}) collective-permute-start(f32[2,1,32,128]{3,2,1,0:T(8,128)S(1)} %get-tuple-element.226), channel_id=1, source_target_pairs={{0,8},{8,16},{16,24},{24,32},{32,40},{40,48},{48,56},{56,64},{64,7... | collective-permute-start | bytes 98312 | tf_op jit(solution)/shard_map/while/body/eval_jaxpr/ppermute | solution.py:18
  16.8 1.0 collective-permute-done.1
  18.2 1.3 collective-permute-start
  19.5 5.2 %collective-permute-start.1 = (f32[2,1,32,128]{3,2,1,0:T(8,128)S(1)}, f32[2,1,32,128]{3,2,1,0:T(8,128)S(1)}, u32[]{:S(2)}, u32[]{:S(2)}) collective-permute-start(f32[2,1,32,128]{3,2,1,0:T(8,128)S(1)} %get-tuple-element.226), channel_id=1, source_target_pairs={{0,8},{8,16},{16,24},{24,32},{32,40},{40,48},{48,56},{56,64},{64,7... | collective-permute-start | bytes 98312 | tf_op jit(solution)/shard_map/while/body/eval_jaxpr/ppermute | solution.py:18
  24.8 1.0 collective-permute-done.1
  26.2 1.3 collective-permute-start
  27.5 5.2 %collective-permute-start.1 = (f32[2,1,32,128]{3,2,1,0:T(8,128)S(1)}, f32[2,1,32,128]{3,2,1,0:T(8,128)S(1)}, u32[]{:S(2)}, u32[]{:S(2)}) collective-permute-start(f32[2,1,32,128]{3,2,1,0:T(8,128)S(1)} %get-tuple-element.226), channel_id=1, source_target_pairs={{0,8},{8,16},{16,24},{24,32},{32,40},{40,48},{48,56},{56,64},{64,7... | collective-permute-start | bytes 98312 | tf_op jit(solution)/shard_map/while/body/eval_jaxpr/ppermute | solution.py:18
  32.7 1.0 collective-permute-done.1
  34.2 1.3 collective-permute-start
  35.5 5.2 %collective-permute-start.1 = (f32[2,1,32,128]{3,2,1,0:T(8,128)S(1)}, f32[2,1,32,128]{3,2,1,0:T(8,128)S(1)}, u32[]{:S(2)}, u32[]{:S(2)}) collective-permute-start(f32[2,1,32,128]{3,2,1,0:T(8,128)S(1)} %get-tuple-element.226), channel_id=1, source_target_pairs={{0,8},{8,16},{16,24},{24,32},{32,40},{40,48},{48,56},{56,64},{64,7... | collective-permute-start | bytes 98312 | tf_op jit(solution)/shard_map/while/body/eval_jaxpr/ppermute | solution.py:18
  40.7 1.0 collective-permute-done.1
  42.1 1.3 collective-permute-start
  43.4 5.2 %collective-permute-start.1 = (f32[2,1,32,128]{3,2,1,0:T(8,128)S(1)}, f32[2,1,32,128]{3,2,1,0:T(8,128)S(1)}, u32[]{:S(2)}, u32[]{:S(2)}) collective-permute-start(f32[2,1,32,128]{3,2,1,0:T(8,128)S(1)} %get-tuple-element.226), channel_id=1, source_target_pairs={{0,8},{8,16},{16,24},{24,32},{32,40},{40,48},{48,56},{56,64},{64,7... | collective-permute-start | bytes 98312 | tf_op jit(solution)/shard_map/while/body/eval_jaxpr/ppermute | solution.py:18
  48.7 1.0 collective-permute-done.1
  50.1 1.3 collective-permute-start
  51.4 5.2 %collective-permute-start.1 = (f32[2,1,32,128]{3,2,1,0:T(8,128)S(1)}, f32[2,1,32,128]{3,2,1,0:T(8,128)S(1)}, u32[]{:S(2)}, u32[]{:S(2)}) collective-permute-start(f32[2,1,32,128]{3,2,1,0:T(8,128)S(1)} %get-tuple-element.226), channel_id=1, source_target_pairs={{0,8},{8,16},{16,24},{24,32},{32,40},{40,48},{48,56},{56,64},{64,7... | collective-permute-start | bytes 98312 | tf_op jit(solution)/shard_map/while/body/eval_jaxpr/ppermute | solution.py:18
  56.6 1.0 collective-permute-done.1
  58.1 1.3 collective-permute-start
  59.4 5.2 %collective-permute-start.1 = (f32[2,1,32,128]{3,2,1,0:T(8,128)S(1)}, f32[2,1,32,128]{3,2,1,0:T(8,128)S(1)}, u32[]{:S(2)}, u32[]{:S(2)}) collective-permute-start(f32[2,1,32,128]{3,2,1,0:T(8,128)S(1)} %get-tuple-element.226), channel_id=1, source_target_pairs={{0,8},{8,16},{16,24},{24,32},{32,40},{40,48},{48,56},{56,64},{64,7... | collective-permute-start | bytes 98312 | tf_op jit(solution)/shard_map/while/body/eval_jaxpr/ppermute | solution.py:18
  64.6 1.0 collective-permute-done.1
  66.0 1.3 collective-permute-start
  67.3 5.3 %collective-permute-start.1 = (f32[2,1,32,128]{3,2,1,0:T(8,128)S(1)}, f32[2,1,32,128]{3,2,1,0:T(8,128)S(1)}, u32[]{:S(2)}, u32[]{:S(2)}) collective-permute-start(f32[2,1,32,128]{3,2,1,0:T(8,128)S(1)} %get-tuple-element.226), channel_id=1, source_target_pairs={{0,8},{8,16},{16,24},{24,32},{32,40},{40,48},{48,56},{56,64},{64,7... | collective-permute-start | bytes 98312 | tf_op jit(solution)/shard_map/while/body/eval_jaxpr/ppermute | solution.py:18
  72.6 1.0 collective-permute-done.1
  74.1 1.3 collective-permute-start
  75.4 5.3 %collective-permute-start.1 = (f32[2,1,32,128]{3,2,1,0:T(8,128)S(1)}, f32[2,1,32,128]{3,2,1,0:T(8,128)S(1)}, u32[]{:S(2)}, u32[]{:S(2)}) collective-permute-start(f32[2,1,32,128]{3,2,1,0:T(8,128)S(1)} %get-tuple-element.226), channel_id=1, source_target_pairs={{0,8},{8,16},{16,24},{24,32},{32,40},{40,48},{48,56},{56,64},{64,7... | collective-permute-start | bytes 98312 | tf_op jit(solution)/shard_map/while/body/eval_jaxpr/ppermute | solution.py:18
  80.8 1.0 collective-permute-done.1
  82.2 1.3 collective-permute-start
  83.5 5.2 %collective-permute-start.1 = (f32[2,1,32,128]{3,2,1,0:T(8,128)S(1)}, f32[2,1,32,128]{3,2,1,0:T(8,128)S(1)}, u32[]{:S(2)}, u32[]{:S(2)}) collective-permute-start(f32[2,1,32,128]{3,2,1,0:T(8,128)S(1)} %get-tuple-element.226), channel_id=1, source_target_pairs={{0,8},{8,16},{16,24},{24,32},{32,40},{40,48},{48,56},{56,64},{64,7... | collective-permute-start | bytes 98312 | tf_op jit(solution)/shard_map/while/body/eval_jaxpr/ppermute | solution.py:18
  88.7 1.0 collective-permute-done.1
  90.2 1.3 collective-permute-start
  91.5 6.5 %collective-permute-start.1 = (f32[2,1,32,128]{3,2,1,0:T(8,128)S(1)}, f32[2,1,32,128]{3,2,1,0:T(8,128)S(1)}, u32[]{:S(2)}, u32[]{:S(2)}) collective-permute-start(f32[2,1,32,128]{3,2,1,0:T(8,128)S(1)} %get-tuple-element.226), channel_id=1, source_target_pairs={{0,8},{8,16},{16,24},{24,32},{32,40},{40,48},{48,56},{56,64},{64,7... | collective-permute-start | bytes 98312 | tf_op jit(solution)/shard_map/while/body/eval_jaxpr/ppermute | solution.py:18
  98.1 1.0 collective-permute-done.1
  99.5 0.8 copy.27
  100.3 20.7 %all-to-all-start = ((f32[2,5,32,128]{3,0,1,2:T(2,128)}), f32[2,5,32,128]{3,0,1,2:T(2,128)S(1)}, u32[]{:S(2)}, u32[]{:S(2)}) async-start(f32[2,5,32,128]{3,0,1,2:T(2,128)} %copy.27), calls=%async_computation | async-start | bytes 327680 | tf_op jit(solution)/shard_map/all_to_all | solution.py:87
  121.2 8.6 %all-to-all-done = f32[2,5,32,128]{3,0,1,2:T(2,128)S(1)} async-done(((f32[2,5,32,128]{3,0,1,2:T(2,128)}), f32[2,5,32,128]{3,0,1,2:T(2,128)S(1)}, u32[]{:S(2)}, u32[]{:S(2)}) %all-to-all-start) | async-done | bytes 163872 | tf_op jit(solution)/shard_map/all_to_all | solution.py:87
  130.4 26.5 %while.23 = (s32[]{:T(128)}, f32[8,32,2560]{2,1,0:T(8,128)S(1)}, f32[8,32,16]{1,0,2:T(8,128)S(1)}, f32[8,32,16]{1,0,2:T(8,128)S(1)}, f32[16,5,4,128]{3,2,1,0:T(4...) while((s32[]{:T(128)}, f32[8,32,2560]{2,1,0:T(8,128)S(1)}, f32[8,32,16]{1,0,2:T(8,128)S(1)}, ...), condition=%wide.wide.region_7.8_spmd, body=%wide.wide.region_3.7_spmd.sunk | while | flops 10404322 | bytes 2648417 | solution.py:91
  130.6 1.2 fusion.17
  131.9 1.8 fusion.18
  133.9 1.2 fusion.17
  135.3 1.8 fusion.18
  137.2 1.2 fusion.17
  138.6 1.8 fusion.18
  140.6 1.2 fusion.17
  141.9 1.8 fusion.18
  143.9 1.2 fusion.17
  145.2 1.8 fusion.18
  147.2 1.2 fusion.17
  148.5 1.8 fusion.18
  150.5 1.2 fusion.17
  151.8 1.8 fusion.18
  153.8 1.2 fusion.17
  155.1 1.8 fusion.18
  157.3 141.2 %pmax.7 = f32[256]{0:T(256)S(1)} all-reduce(f32[256]{0:T(256)S(1)} %reduce_max.12), channel_id=1, replica_groups=mesh['space'=64,'sta'=8] {'space','sta'}, use_global_device_ids=true, to_apply=%region_9.10 | all-reduce | flops 256 | bytes 2048 | tf_op jit(solution)/shard_map/pmax | solution.py:97
  298.5 2.0 exponential_reduce_fusion
  300.5 2.8 div.34
  303.4 94.4 %psum.7 = f32[256]{0:T(256)S(1)} all-reduce(f32[256]{0:T(256)S(1)} %reduce_sum.49), channel_id=1, replica_groups=mesh['space'=64,'sta'=8] {'space','sta'}, use_global_device_ids=true, to_apply=%region_11.12 | all-reduce | flops 256 | bytes 2048 | tf_op jit(solution)/shard_map/psum | solution.py:99
  397.8 2.5 exponential_divide_fusion
  (149 shorter events, 9.4 us)
Async XLA Ops:
  3.1 117.9 %copy-start.2 = (s32[256,16]{0,1:T(8,128)S(1)}, s32[256,16]{0,1:T(8,128)}, u32[]{:S(2)}) copy-start(s32[256,16]{0,1:T(8,128)} %param.13) | copy-start | bytes 49156
  3.1 118.0 %copy-start.1 = (f32[256,16]{0,1:T(8,128)S(1)}, f32[256,16]{0,1:T(8,128)}, u32[]{:S(2)}) copy-start(f32[256,16]{0,1:T(8,128)} %param.12) | copy-start | bytes 49156
  3.1 6.0 %collective-permute-start = (f32[2,1,32,128]{3,2,1,0:T(8,128)S(1)}, f32[2,1,32,128]{3,2,1,0:T(8,128)S(1)}, u32[]{:S(2)}, u32[]{:S(2)}) collective-permute-start(f32[2,1,32,128]{3,2,1,0:T(8,128)S(1)} %get-tuple-element.225), channel_id=1, source_target_pairs={{8,0},{16,8},{24,16},{32,24},{40,32},{48,40},{56,48},{64,56},{72,6... | collective-permute-start | bytes 98312 | tf_op jit(solution)/shard_map/while/body/eval_jaxpr/ppermute | solution.py:21
  4.4 5.7 %collective-permute-start.1 = (f32[2,1,32,128]{3,2,1,0:T(8,128)S(1)}, f32[2,1,32,128]{3,2,1,0:T(8,128)S(1)}, u32[]{:S(2)}, u32[]{:S(2)}) collective-permute-start(f32[2,1,32,128]{3,2,1,0:T(8,128)S(1)} %get-tuple-element.226), channel_id=1, source_target_pairs={{0,8},{8,16},{16,24},{24,32},{32,40},{40,48},{48,56},{56,64},{64,7... | collective-permute-start | bytes 98312 | tf_op jit(solution)/shard_map/while/body/eval_jaxpr/ppermute | solution.py:18
  10.6 6.2 %collective-permute-start = (f32[2,1,32,128]{3,2,1,0:T(8,128)S(1)}, f32[2,1,32,128]{3,2,1,0:T(8,128)S(1)}, u32[]{:S(2)}, u32[]{:S(2)}) collective-permute-start(f32[2,1,32,128]{3,2,1,0:T(8,128)S(1)} %get-tuple-element.225), channel_id=1, source_target_pairs={{8,0},{16,8},{24,16},{32,24},{40,32},{48,40},{56,48},{64,56},{72,6... | collective-permute-start | bytes 98312 | tf_op jit(solution)/shard_map/while/body/eval_jaxpr/ppermute | solution.py:21
  11.9 5.9 %collective-permute-start.1 = (f32[2,1,32,128]{3,2,1,0:T(8,128)S(1)}, f32[2,1,32,128]{3,2,1,0:T(8,128)S(1)}, u32[]{:S(2)}, u32[]{:S(2)}) collective-permute-start(f32[2,1,32,128]{3,2,1,0:T(8,128)S(1)} %get-tuple-element.226), channel_id=1, source_target_pairs={{0,8},{8,16},{16,24},{24,32},{32,40},{40,48},{48,56},{56,64},{64,7... | collective-permute-start | bytes 98312 | tf_op jit(solution)/shard_map/while/body/eval_jaxpr/ppermute | solution.py:18
  18.2 6.5 %collective-permute-start = (f32[2,1,32,128]{3,2,1,0:T(8,128)S(1)}, f32[2,1,32,128]{3,2,1,0:T(8,128)S(1)}, u32[]{:S(2)}, u32[]{:S(2)}) collective-permute-start(f32[2,1,32,128]{3,2,1,0:T(8,128)S(1)} %get-tuple-element.225), channel_id=1, source_target_pairs={{8,0},{16,8},{24,16},{32,24},{40,32},{48,40},{56,48},{64,56},{72,6... | collective-permute-start | bytes 98312 | tf_op jit(solution)/shard_map/while/body/eval_jaxpr/ppermute | solution.py:21
  19.5 6.2 %collective-permute-start.1 = (f32[2,1,32,128]{3,2,1,0:T(8,128)S(1)}, f32[2,1,32,128]{3,2,1,0:T(8,128)S(1)}, u32[]{:S(2)}, u32[]{:S(2)}) collective-permute-start(f32[2,1,32,128]{3,2,1,0:T(8,128)S(1)} %get-tuple-element.226), channel_id=1, source_target_pairs={{0,8},{8,16},{16,24},{24,32},{32,40},{40,48},{48,56},{56,64},{64,7... | collective-permute-start | bytes 98312 | tf_op jit(solution)/shard_map/while/body/eval_jaxpr/ppermute | solution.py:18
  26.2 6.5 %collective-permute-start = (f32[2,1,32,128]{3,2,1,0:T(8,128)S(1)}, f32[2,1,32,128]{3,2,1,0:T(8,128)S(1)}, u32[]{:S(2)}, u32[]{:S(2)}) collective-permute-start(f32[2,1,32,128]{3,2,1,0:T(8,128)S(1)} %get-tuple-element.225), channel_id=1, source_target_pairs={{8,0},{16,8},{24,16},{32,24},{40,32},{48,40},{56,48},{64,56},{72,6... | collective-permute-start | bytes 98312 | tf_op jit(solution)/shard_map/while/body/eval_jaxpr/ppermute | solution.py:21
  27.5 6.2 %collective-permute-start.1 = (f32[2,1,32,128]{3,2,1,0:T(8,128)S(1)}, f32[2,1,32,128]{3,2,1,0:T(8,128)S(1)}, u32[]{:S(2)}, u32[]{:S(2)}) collective-permute-start(f32[2,1,32,128]{3,2,1,0:T(8,128)S(1)} %get-tuple-element.226), channel_id=1, source_target_pairs={{0,8},{8,16},{16,24},{24,32},{32,40},{40,48},{48,56},{56,64},{64,7... | collective-permute-start | bytes 98312 | tf_op jit(solution)/shard_map/while/body/eval_jaxpr/ppermute | solution.py:18
  34.2 6.5 %collective-permute-start = (f32[2,1,32,128]{3,2,1,0:T(8,128)S(1)}, f32[2,1,32,128]{3,2,1,0:T(8,128)S(1)}, u32[]{:S(2)}, u32[]{:S(2)}) collective-permute-start(f32[2,1,32,128]{3,2,1,0:T(8,128)S(1)} %get-tuple-element.225), channel_id=1, source_target_pairs={{8,0},{16,8},{24,16},{32,24},{40,32},{48,40},{56,48},{64,56},{72,6... | collective-permute-start | bytes 98312 | tf_op jit(solution)/shard_map/while/body/eval_jaxpr/ppermute | solution.py:21
  35.5 6.2 %collective-permute-start.1 = (f32[2,1,32,128]{3,2,1,0:T(8,128)S(1)}, f32[2,1,32,128]{3,2,1,0:T(8,128)S(1)}, u32[]{:S(2)}, u32[]{:S(2)}) collective-permute-start(f32[2,1,32,128]{3,2,1,0:T(8,128)S(1)} %get-tuple-element.226), channel_id=1, source_target_pairs={{0,8},{8,16},{16,24},{24,32},{32,40},{40,48},{48,56},{56,64},{64,7... | collective-permute-start | bytes 98312 | tf_op jit(solution)/shard_map/while/body/eval_jaxpr/ppermute | solution.py:18
  42.1 6.5 %collective-permute-start = (f32[2,1,32,128]{3,2,1,0:T(8,128)S(1)}, f32[2,1,32,128]{3,2,1,0:T(8,128)S(1)}, u32[]{:S(2)}, u32[]{:S(2)}) collective-permute-start(f32[2,1,32,128]{3,2,1,0:T(8,128)S(1)} %get-tuple-element.225), channel_id=1, source_target_pairs={{8,0},{16,8},{24,16},{32,24},{40,32},{48,40},{56,48},{64,56},{72,6... | collective-permute-start | bytes 98312 | tf_op jit(solution)/shard_map/while/body/eval_jaxpr/ppermute | solution.py:21
  43.4 6.2 %collective-permute-start.1 = (f32[2,1,32,128]{3,2,1,0:T(8,128)S(1)}, f32[2,1,32,128]{3,2,1,0:T(8,128)S(1)}, u32[]{:S(2)}, u32[]{:S(2)}) collective-permute-start(f32[2,1,32,128]{3,2,1,0:T(8,128)S(1)} %get-tuple-element.226), channel_id=1, source_target_pairs={{0,8},{8,16},{16,24},{24,32},{32,40},{40,48},{48,56},{56,64},{64,7... | collective-permute-start | bytes 98312 | tf_op jit(solution)/shard_map/while/body/eval_jaxpr/ppermute | solution.py:18
  50.1 6.5 %collective-permute-start = (f32[2,1,32,128]{3,2,1,0:T(8,128)S(1)}, f32[2,1,32,128]{3,2,1,0:T(8,128)S(1)}, u32[]{:S(2)}, u32[]{:S(2)}) collective-permute-start(f32[2,1,32,128]{3,2,1,0:T(8,128)S(1)} %get-tuple-element.225), channel_id=1, source_target_pairs={{8,0},{16,8},{24,16},{32,24},{40,32},{48,40},{56,48},{64,56},{72,6... | collective-permute-start | bytes 98312 | tf_op jit(solution)/shard_map/while/body/eval_jaxpr/ppermute | solution.py:21
  51.4 6.2 %collective-permute-start.1 = (f32[2,1,32,128]{3,2,1,0:T(8,128)S(1)}, f32[2,1,32,128]{3,2,1,0:T(8,128)S(1)}, u32[]{:S(2)}, u32[]{:S(2)}) collective-permute-start(f32[2,1,32,128]{3,2,1,0:T(8,128)S(1)} %get-tuple-element.226), channel_id=1, source_target_pairs={{0,8},{8,16},{16,24},{24,32},{32,40},{40,48},{48,56},{56,64},{64,7... | collective-permute-start | bytes 98312 | tf_op jit(solution)/shard_map/while/body/eval_jaxpr/ppermute | solution.py:18
  58.1 6.5 %collective-permute-start = (f32[2,1,32,128]{3,2,1,0:T(8,128)S(1)}, f32[2,1,32,128]{3,2,1,0:T(8,128)S(1)}, u32[]{:S(2)}, u32[]{:S(2)}) collective-permute-start(f32[2,1,32,128]{3,2,1,0:T(8,128)S(1)} %get-tuple-element.225), channel_id=1, source_target_pairs={{8,0},{16,8},{24,16},{32,24},{40,32},{48,40},{56,48},{64,56},{72,6... | collective-permute-start | bytes 98312 | tf_op jit(solution)/shard_map/while/body/eval_jaxpr/ppermute | solution.py:21
  59.4 6.2 %collective-permute-start.1 = (f32[2,1,32,128]{3,2,1,0:T(8,128)S(1)}, f32[2,1,32,128]{3,2,1,0:T(8,128)S(1)}, u32[]{:S(2)}, u32[]{:S(2)}) collective-permute-start(f32[2,1,32,128]{3,2,1,0:T(8,128)S(1)} %get-tuple-element.226), channel_id=1, source_target_pairs={{0,8},{8,16},{16,24},{24,32},{32,40},{40,48},{48,56},{56,64},{64,7... | collective-permute-start | bytes 98312 | tf_op jit(solution)/shard_map/while/body/eval_jaxpr/ppermute | solution.py:18
  66.0 6.6 %collective-permute-start = (f32[2,1,32,128]{3,2,1,0:T(8,128)S(1)}, f32[2,1,32,128]{3,2,1,0:T(8,128)S(1)}, u32[]{:S(2)}, u32[]{:S(2)}) collective-permute-start(f32[2,1,32,128]{3,2,1,0:T(8,128)S(1)} %get-tuple-element.225), channel_id=1, source_target_pairs={{8,0},{16,8},{24,16},{32,24},{40,32},{48,40},{56,48},{64,56},{72,6... | collective-permute-start | bytes 98312 | tf_op jit(solution)/shard_map/while/body/eval_jaxpr/ppermute | solution.py:21
  67.3 6.3 %collective-permute-start.1 = (f32[2,1,32,128]{3,2,1,0:T(8,128)S(1)}, f32[2,1,32,128]{3,2,1,0:T(8,128)S(1)}, u32[]{:S(2)}, u32[]{:S(2)}) collective-permute-start(f32[2,1,32,128]{3,2,1,0:T(8,128)S(1)} %get-tuple-element.226), channel_id=1, source_target_pairs={{0,8},{8,16},{16,24},{24,32},{32,40},{40,48},{48,56},{56,64},{64,7... | collective-permute-start | bytes 98312 | tf_op jit(solution)/shard_map/while/body/eval_jaxpr/ppermute | solution.py:18
  74.1 6.7 %collective-permute-start = (f32[2,1,32,128]{3,2,1,0:T(8,128)S(1)}, f32[2,1,32,128]{3,2,1,0:T(8,128)S(1)}, u32[]{:S(2)}, u32[]{:S(2)}) collective-permute-start(f32[2,1,32,128]{3,2,1,0:T(8,128)S(1)} %get-tuple-element.225), channel_id=1, source_target_pairs={{8,0},{16,8},{24,16},{32,24},{40,32},{48,40},{56,48},{64,56},{72,6... | collective-permute-start | bytes 98312 | tf_op jit(solution)/shard_map/while/body/eval_jaxpr/ppermute | solution.py:21
  75.4 6.4 %collective-permute-start.1 = (f32[2,1,32,128]{3,2,1,0:T(8,128)S(1)}, f32[2,1,32,128]{3,2,1,0:T(8,128)S(1)}, u32[]{:S(2)}, u32[]{:S(2)}) collective-permute-start(f32[2,1,32,128]{3,2,1,0:T(8,128)S(1)} %get-tuple-element.226), channel_id=1, source_target_pairs={{0,8},{8,16},{16,24},{24,32},{32,40},{40,48},{48,56},{56,64},{64,7... | collective-permute-start | bytes 98312 | tf_op jit(solution)/shard_map/while/body/eval_jaxpr/ppermute | solution.py:18
  82.2 6.5 %collective-permute-start = (f32[2,1,32,128]{3,2,1,0:T(8,128)S(1)}, f32[2,1,32,128]{3,2,1,0:T(8,128)S(1)}, u32[]{:S(2)}, u32[]{:S(2)}) collective-permute-start(f32[2,1,32,128]{3,2,1,0:T(8,128)S(1)} %get-tuple-element.225), channel_id=1, source_target_pairs={{8,0},{16,8},{24,16},{32,24},{40,32},{48,40},{56,48},{64,56},{72,6... | collective-permute-start | bytes 98312 | tf_op jit(solution)/shard_map/while/body/eval_jaxpr/ppermute | solution.py:21
  83.5 6.2 %collective-permute-start.1 = (f32[2,1,32,128]{3,2,1,0:T(8,128)S(1)}, f32[2,1,32,128]{3,2,1,0:T(8,128)S(1)}, u32[]{:S(2)}, u32[]{:S(2)}) collective-permute-start(f32[2,1,32,128]{3,2,1,0:T(8,128)S(1)} %get-tuple-element.226), channel_id=1, source_target_pairs={{0,8},{8,16},{16,24},{24,32},{32,40},{40,48},{48,56},{56,64},{64,7... | collective-permute-start | bytes 98312 | tf_op jit(solution)/shard_map/while/body/eval_jaxpr/ppermute | solution.py:18
  90.2 7.9 %collective-permute-start = (f32[2,1,32,128]{3,2,1,0:T(8,128)S(1)}, f32[2,1,32,128]{3,2,1,0:T(8,128)S(1)}, u32[]{:S(2)}, u32[]{:S(2)}) collective-permute-start(f32[2,1,32,128]{3,2,1,0:T(8,128)S(1)} %get-tuple-element.225), channel_id=1, source_target_pairs={{8,0},{16,8},{24,16},{32,24},{40,32},{48,40},{56,48},{64,56},{72,6... | collective-permute-start | bytes 98312 | tf_op jit(solution)/shard_map/while/body/eval_jaxpr/ppermute | solution.py:21
  91.5 7.5 %collective-permute-start.1 = (f32[2,1,32,128]{3,2,1,0:T(8,128)S(1)}, f32[2,1,32,128]{3,2,1,0:T(8,128)S(1)}, u32[]{:S(2)}, u32[]{:S(2)}) collective-permute-start(f32[2,1,32,128]{3,2,1,0:T(8,128)S(1)} %get-tuple-element.226), channel_id=1, source_target_pairs={{0,8},{8,16},{16,24},{24,32},{32,40},{40,48},{48,56},{56,64},{64,7... | collective-permute-start | bytes 98312 | tf_op jit(solution)/shard_map/while/body/eval_jaxpr/ppermute | solution.py:18
  100.3 29.5 %all-to-all-start = ((f32[2,5,32,128]{3,0,1,2:T(2,128)}), f32[2,5,32,128]{3,0,1,2:T(2,128)S(1)}, u32[]{:S(2)}, u32[]{:S(2)}) async-start(f32[2,5,32,128]{3,0,1,2:T(2,128)} %copy.27), calls=%async_computation | async-start | bytes 327680 | tf_op jit(solution)/shard_map/all_to_all | solution.py:87
  129.8 0.7 copy-start
where the time goes:
time: 401 us; the launch traced here: 400 us
  blocking collectives  236 us (59%)
  starting transfers between devices  99.1 us (25%)
  other arithmetic  36.1 us (9%)
  waiting for transfers between devices  20.1 us (5%)
  local copies, waits for them, and re-layouts  7.41 us (2%)
    pmax x1, blocking collectives, body(): top_score = lax.pmax(local_top, ('space', 'sta'))  141 us
    psum x1, blocking collectives, body(): mass_sum = lax.psum(jnp.sum(cell_weights, 1), ('space', 'sta'))  94.4 us
    ppermute x12, starting transfers between devices, extended_2(): lax.ppermute(lax.slice_in_dim(block, block.shape[dim] - width, None, axis...  62.9 us
    all_to_all x1, starting transfers between devices, body(): lax.all_to_all(tables, 'sta', split_axis=2, concat_axis=0, tiled=True)  20.7 us
    ppermute x12, starting transfers between devices, extended_2(): lax.ppermute(lax.slice_in_dim(block, 0, width, axis=dim), axis, backward)  15.5 us
    reduce_sum x8, other arithmetic, misfit_block(): return jnp.sum(observed[:, :, None] * deviation * deviation, 1)  14 us
    ppermute x12, waiting for transfers between devices, extended_2(): lax.ppermute(lax.slice_in_dim(block, block.shape[dim] - width, None, axis...  11.5 us
    reduce_sum x8, other arithmetic, misfit_block(): jnp.sum(observed[:, :, None] * residual, 1) / pick_count[:, None]  9.54 us
  transfers between devices with their start and end apart: 25, of which 13 were waited for; matrix products, arithmetic and copies ran while one was open for 0% of the time, Pallas kernels for 0%

commit v1 on v0

--- a/solution.py
+++ b/solution.py
@@ -96,7 +96,7 @@
     local_top = jnp.max(score, 1)
     top_score = lax.pmax(local_top, ("space", "sta"))
     cell_weights = jnp.exp(score - top_score[:, None])
-    mass_sum = lax.psum(jnp.sum(cell_weights, 1), ("space", "sta"))
+    mass_sum = jnp.sum(lax.all_gather(jnp.sum(cell_weights, 1), ("space", "sta")), axis=0)
     density = cell_weights / mass_sum[:, None]
     density = density.reshape(picks.shape[0], refined.shape[1], refined.shape[2], refined.shape[3])
     return (refined, density)

time: 401 us -> 989 us (2.47)
  blocking collectives: 236 us -> 823 us
    all_gather x0 -> x1, blocking collectives: none -> 681 us  [body(): lax.all_gather(jnp.sum(cell_weights, 1), ('space', 'sta'))]
    psum x1 -> x0, blocking collectives: 94.4 us -> none  [body(): mass_sum = lax.psum(jnp.sum(cell_weights, 1), ('space', 'sta'))]
where the time goes in v1:
time: 989 us; the launch traced here: 988 us
  blocking collectives  823 us (83%)
  starting transfers between devices  99.1 us (10%)
  other arithmetic  36.7 us (4%)
  waiting for transfers between devices  20.1 us (2%)
    all_gather x1, blocking collectives, body(): lax.all_gather(jnp.sum(cell_weights, 1), ('space', 'sta'))  681 us
    pmax x1, blocking collectives, body(): top_score = lax.pmax(local_top, ('space', 'sta'))  141 us
    ppermute x12, starting transfers between devices, extended_2(): lax.ppermute(lax.slice_in_dim(block, block.shape[dim] - width, None, axis...  62.9 us
    all_to_all x1, starting transfers between devices, body(): lax.all_to_all(tables, 'sta', split_axis=2, concat_axis=0, tiled=True)  20.7 us
  transfers between devices with their start and end apart: 25, of which 13 were waited for; matrix products, arithmetic and copies ran while one was open for 0% of the time, Pallas kernels for 0%

profile of v1, /device:TPU:1, one launch (start us, length us, event | category | flops | bytes accessed | tf_op | source)
XLA Modules:
  0.0 987.9 jit_solution(10884797477162262183)
XLA Ops:
  0.6 0.9 copy.54
  1.5 1.5 select_reduce_fusion
  3.1 96.4 %while.22 = (s32[]{:T(128)}, f32[2,5,32,128]{3,2,1,0:T(8,128)S(1)}, pred[]{:T(512)}, pred[]{:T(512)}, f32[5,32,128]{2,1,0:T(8,128)S(1)}, /*index=5*/f32[1,5,32,128]{3,2,1,0:T(8,128)S(1)}, s32[]{:T(128)}) while((s32[]{:T(128)}, f32[2,5,32,128]{3,2,1,0:T(8,128)S(1)}, pred[]{:T(512)}, pred[]{:T(512)}, f32[5,32,128]{2,1,0:T(8,128)S(1)}, ...), condition=%wide.region_2.3_spmd, body=%wide.region_1.2_spmd.sunk | while | flops 1523749 | bytes 2244781 | solution.py:86
  3.1 1.3 collective-permute-start
  4.4 4.6 collective-permute-start.1
  9.1 1.0 collective-permute-done.1
  10.6 1.3 collective-permute-start
  11.9 4.9 collective-permute-start.1
  16.8 1.0 collective-permute-done.1
  18.2 1.3 collective-permute-start
  19.5 5.2 collective-permute-start.1
  24.8 1.0 collective-permute-done.1
  26.2 1.3 collective-permute-start
  27.5 5.2 collective-permute-start.1
  32.7 1.0 collective-permute-done.1
  34.2 1.3 collective-permute-start
  35.5 5.2 collective-permute-start.1
  40.7 1.0 collective-permute-done.1
  42.1 1.3 collective-permute-start
  43.4 5.2 collective-permute-start.1
  48.7 1.0 collective-permute-done.1
  50.1 1.3 collective-permute-start
  51.4 5.2 collective-permute-start.1
  56.6 1.0 collective-permute-done.1
  58.1 1.3 collective-permute-start
  59.4 5.2 collective-permute-start.1
  64.6 1.0 collective-permute-done.1
  66.0 1.3 collective-permute-start
  67.3 5.3 collective-permute-start.1
  72.6 1.0 collective-permute-done.1
  74.1 1.3 collective-permute-start
  75.4 5.3 collective-permute-start.1
  80.8 1.0 collective-permute-done.1
  82.2 1.3 collective-permute-start
  83.5 5.2 collective-permute-start.1
  88.7 1.0 collective-permute-done.1
  90.2 1.3 collective-permute-start
  91.5 6.5 collective-permute-start.1
  98.1 1.0 collective-permute-done.1
  99.5 0.8 copy.27
  100.3 20.7 %all-to-all-start = ((f32[2,5,32,128]{3,0,1,2:T(2,128)}), f32[2,5,32,128]{3,0,1,2:T(2,128)S(1)}, u32[]{:S(2)}, u32[]{:S(2)}) async-start(f32[2,5,32,128]{3,0,1,2:T(2,128)} %copy.27), calls=%async_computation | async-start | bytes 327680 | tf_op jit(solution)/shard_map/all_to_all | solution.py:87
  121.2 8.6 all-to-all-done
  130.4 26.5 %while.23 = (s32[]{:T(128)}, f32[8,32,2560]{2,1,0:T(8,128)S(1)}, f32[8,32,16]{1,0,2:T(8,128)S(1)}, f32[8,32,16]{1,0,2:T(8,128)S(1)}, f32[16,5,4,128]{3,2,1,0:T(4...) while((s32[]{:T(128)}, f32[8,32,2560]{2,1,0:T(8,128)S(1)}, f32[8,32,16]{1,0,2:T(8,128)S(1)}, ...), condition=%wide.wide.region_7.8_spmd, body=%wide.wide.region_3.7_spmd.sunk | while | flops 10404322 | bytes 2648417 | solution.py:91
  130.6 1.2 fusion.17
  131.9 1.8 fusion.18
  133.9 1.2 fusion.17
  135.3 1.8 fusion.18
  137.2 1.2 fusion.17
  138.6 1.8 fusion.18
  140.6 1.2 fusion.17
  141.9 1.8 fusion.18
  143.9 1.2 fusion.17
  145.2 1.8 fusion.18
  147.2 1.2 fusion.17
  148.5 1.8 fusion.18
  150.5 1.2 fusion.17
  151.8 1.8 fusion.18
  153.8 1.2 fusion.17
  155.1 1.8 fusion.18
  157.3 141.2 %pmax.7 = f32[256]{0:T(256)S(1)} all-reduce(f32[256]{0:T(256)S(1)} %reduce_max.12), channel_id=1, replica_groups=mesh['space'=64,'sta'=8] {'space','sta'}, use_global_device_ids=true, to_apply=%region_9.10 | all-reduce | flops 256 | bytes 2048 | tf_op jit(solution)/shard_map/pmax | solution.py:97
  298.5 2.0 exponential_reduce_fusion
  300.5 2.8 div.34
  303.4 681.3 %all-gather = f32[512,1,256]{2,1,0:T(1,128)S(1)} all-gather(f32[1,1,256]{2,1,0:T(1,128)S(1)} %reshape.91), channel_id=1, replica_groups=mesh['space'=64,'sta'=8] {'space','sta'}, dimensions={0}, use_global_device_ids=true | all-gather | bytes 525312 | tf_op jit(solution)/shard_map/all_gather | solution.py:99
  985.3 2.6 exponential_divide_fusion
  (150 shorter events, 10.0 us)
Async XLA Ops:
  3.1 117.9 %copy-start.2 = (s32[256,16]{0,1:T(8,128)S(1)}, s32[256,16]{0,1:T(8,128)}, u32[]{:S(2)}) copy-start(s32[256,16]{0,1:T(8,128)} %param.13) | copy-start | bytes 49156
  3.1 118.0 %copy-start.1 = (f32[256,16]{0,1:T(8,128)S(1)}, f32[256,16]{0,1:T(8,128)}, u32[]{:S(2)}) copy-start(f32[256,16]{0,1:T(8,128)} %param.12) | copy-start | bytes 49156
  3.1 6.0 collective-permute-start
  4.4 5.7 collective-permute-start.1
  10.6 6.2 collective-permute-start
  11.9 5.9 collective-permute-start.1
  18.2 6.5 collective-permute-start
  19.5 6.2 collective-permute-start.1
  26.2 6.5 collective-permute-start
  27.5 6.2 collective-permute-start.1
  34.2 6.5 collective-permute-start
  35.5 6.2 collective-permute-start.1
  42.1 6.5 collective-permute-start
  43.4 6.2 collective-permute-start.1
  50.1 6.5 collective-permute-start
  51.4 6.2 collective-permute-start.1
  58.1 6.5 collective-permute-start
  59.4 6.2 collective-permute-start.1
  66.0 6.6 collective-permute-start
  67.3 6.3 collective-permute-start.1
  74.1 6.7 collective-permute-start
  75.4 6.4 collective-permute-start.1
  82.2 6.5 collective-permute-start
  83.5 6.2 collective-permute-start.1
  90.2 7.9 collective-permute-start
  91.5 7.5 collective-permute-start.1
  100.3 29.5 %all-to-all-start = ((f32[2,5,32,128]{3,0,1,2:T(2,128)}), f32[2,5,32,128]{3,0,1,2:T(2,128)S(1)}, u32[]{:S(2)}, u32[]{:S(2)}) async-start(f32[2,5,32,128]{3,0,1,2:T(2,128)} %copy.27), calls=%async_computation | async-start | bytes 327680 | tf_op jit(solution)/shard_map/all_to_all | solution.py:87
  129.8 0.7 copy-start
